TPU v7x, 32 devices: a whole 2x2x4 slice. The times are simulated.
32 devices in a mesh: tm: 16 (over z, y, x), row: 2 (over core).
Axes of the slice: x: 2, y: 2, z: 4, core: 2. Of those that a mesh axis runs over, the one named last changes fastest.
Arguments:
- initial: float32 [1024], replicated, may hold values from -6 to 6
- dynamics: float32 [1024, 1024], replicated, may hold values from -0.009765625 to 0.009765625
- obs_rows: bfloat16 [32768, 1024], P('tm', 'row'), may hold values from -0.1875 to 0.1875
- obs_values: bfloat16 [32768], P('tm'), may hold values from -6 to 6
- obs_slab: int32 [32768, 1], P('tm'), may hold values from 0 to 31; in each aligned block of 2048 rows (0 to 2047, 2048 to 4095, ...) at most 64 rows name the same one
Outputs:
- states: float32 [32, 1024], P('tm', 'row')
Inputs may be any that keep to these rules, and one draw needn't show every extreme that they name: `obs_slab`: within the rows ingested by one index of tm, no slab is named by more than 64 rows, a bound that some block reaches of them.
All inputs are finite; a program needn't handle non-finite values.
Results may differ from a plain program's by a relative error of at most 0.0003.
Values may be sent and summed in bfloat16 or wider, within the bound.
A program may use at most 128 MiB of HBM per device.

v0:
```python
import jax
import jax.numpy as jnp
from jax import lax
from jax.sharding import PartitionSpec as P

SLAB_DEV = 2
CAP = 64
sigma_gain = 0.3


def shifted(value, axis, steps):
    count = lax.axis_size(axis)
    first, last = (max(0, -steps), min(count, count - steps))
    return lax.ppermute(value, axis, [(source, source + steps) for source in range(first, last)])


def left_product(left_rows, pieces):
    new_matrix = jnp.dot(left_rows, pieces[0], precision=lax.Precision.HIGHEST)
    new_vector = jnp.dot(left_rows, pieces[1], precision=lax.Precision.HIGHEST)
    return (new_matrix, new_vector)


def body(initial, dynamics, obs_rows, obs_values, obs_slab):
    time_devs = lax.axis_size("tm")
    row_devs = lax.axis_size("row")
    state_width = dynamics.shape[1]
    local_cols = state_width // row_devs
    row_start = lax.axis_index("row") * local_cols
    time_index = lax.axis_index("tm")
    capacity = CAP
    slab_total = SLAB_DEV * time_devs
    obs_count = obs_rows.shape[0]
    target = obs_slab[:, 0]
    onehot = (target[:, None] == jnp.arange(slab_total, dtype=jnp.int32)[None, :]).astype(jnp.int32)
    rank_in = jnp.sum(onehot * (jnp.cumsum(onehot, axis=0) - 1), axis=1)
    owner_dev = target // SLAB_DEV
    within = target % SLAB_DEV
    slot_index = (within * time_devs + owner_dev) * capacity + rank_in
    slot_table = (
        jnp.full((slab_total * capacity,), obs_count, jnp.int32)
        .at[slot_index]
        .set(jnp.arange(obs_count, dtype=jnp.int32))
    )
    padded_rows = jnp.concatenate([obs_rows, jnp.zeros((1, local_cols), jnp.bfloat16)], axis=0)
    padded_values = jnp.concatenate([obs_values, jnp.zeros((1,), jnp.bfloat16)], axis=0)
    send_rows = padded_rows[slot_table].reshape(SLAB_DEV, time_devs, capacity, local_cols)
    send_values = padded_values[slot_table].reshape(SLAB_DEV, time_devs, capacity)
    recv_rows, recv_values = (
        lax.all_to_all(send_rows, "tm", split_axis=1, concat_axis=1, tiled=True),
        lax.all_to_all(send_values, "tm", split_axis=1, concat_axis=1, tiled=True),
    )
    slab_rows = recv_rows.reshape(SLAB_DEV, time_devs * capacity, local_cols)
    slab_values = recv_values.reshape(SLAB_DEV, time_devs * capacity)
    information = jnp.einsum(
        "sra,srb->sab",
        slab_rows,
        lax.all_gather(slab_rows, "row", axis=2, tiled=True),
        preferred_element_type=jnp.float32,
    )
    moment = jnp.einsum("sr,sra->sa", slab_values, slab_rows, preferred_element_type=jnp.float32)
    evolve = jnp.eye(state_width, dtype=jnp.float32) + dynamics
    evolve_rows = lax.dynamic_slice_in_dim(evolve, row_start, local_cols, 0)
    transitions = []
    offsets = []
    for slab_index in range(SLAB_DEV):
        transitions.append(
            evolve_rows
            - sigma_gain * jnp.dot(information[slab_index], evolve, precision=lax.Precision.HIGHEST)
        )
        offsets.append(sigma_gain * moment[slab_index])
    composed = transitions[0]
    composed_offset = offsets[0]
    slab_index = 1
    new_matrix, new_vector = left_product(
        transitions[slab_index],
        (
            lax.all_gather(composed, "row", axis=0, tiled=True),
            lax.all_gather(composed_offset, "row", axis=0, tiled=True),
        ),
    )
    composed = new_matrix
    composed_offset = new_vector + offsets[slab_index]
    initial_rows = lax.dynamic_slice_in_dim(initial, row_start, local_cols, 0)

    def advance(turn, state_rows):
        whole_state = lax.all_gather(state_rows, "row", axis=0, tiled=True)
        leaving = jnp.dot(composed, whole_state, precision=lax.Precision.HIGHEST) + composed_offset
        arriving = shifted(leaving, "tm", 1)
        return jnp.where(time_index == 0, initial_rows, arriving)

    entry_rows = lax.fori_loop(0, time_devs - 1, advance, initial_rows)
    states = []
    current = entry_rows
    for slab_index in range(SLAB_DEV):
        whole_state = lax.all_gather(current, "row", axis=0, tiled=True)
        current = (
            jnp.dot(transitions[slab_index], whole_state, precision=lax.Precision.HIGHEST)
            + offsets[slab_index]
        )
        states.append(current)
    return jnp.stack(states)


def solution(mesh):
    placed = (P(), P(), P("tm", "row"), P("tm"), P("tm", None))
    return jax.shard_map(
        body, mesh=mesh, in_specs=placed, out_specs=P("tm", "row"), check_vma=False
    )
```

profile of v0, /device:TPU:9, one launch (start us, length us, event | category | flops | bytes accessed | tf_op | source)
XLA Modules:
  0.0 357.0 jit_solution(5598932367776925572)
XLA Ops:
  7.3 9.1 %reduce-window.6 = s32[32,16,128]{2,1,0:T(8,128)S(1)} reduce-window(s32[32,16,128]{2,1,0:T(8,128)S(1)} %fusion.4, s32[]{:T(128)} %copy.37), window={size=1x1x128 pad=0_0x0_0x127_0}, to_apply=%region_0.0 | reduce-window | flops 8323072 | bytes 524292 | tf_op jit(solution)/shard_map/reduce-window
  17.3 8.0 %scatter_custom_fusion = s32[2048]{0:T(1024)S(1)} fusion(s32[2048]{0:T(1024)S(1)} %bitcast.110, s32[2048]{0:T(1024)S(1)} %iota.23, s32[]{:T(128)} %constant.63.clone.1), kind=kCustom, calls=%fused_computation.34 | custom fusion | bytes 8196 | tf_op jit(solution)/shard_map/scatter | solution.py:42
  27.1 9.2 %gather_fusion = bf16[2048,512]{1,0:T(8,128)(2,1)} fusion(bf16[2049,512]{1,0:T(8,128)(2,1)S(1)} %concatenate.6, s32[2048]{0:T(1024)S(1)} %fusion.5), kind=kCustom, calls=%fused_computation | custom fusion | bytes 4202496 | tf_op jit(solution)/shard_map/gather | solution.py:46
  38.2 53.8 %all_to_all.10 = bf16[2,16,64,512]{3,2,0,1:T(8,128)(2,1)S(1)} all-to-all(bf16[2,16,64,512]{3,2,0,1:T(8,128)(2,1)S(1)} %copy.17), channel_id=1, replica_groups=mesh['tm'=16,'row'=2] {'tm'}, dimensions={1} | all-to-all | bytes 4194304 | tf_op jit(solution)/shard_map/all_to_all | solution.py:49
  93.7 5.0 %convert_add_fusion = f32[1024,1024]{1,0:T(8,128)} fusion(f32[1024,1024]{1,0:T(8,128)} %param.8), kind=kLoop, calls=%fused_computation.4 | loop fusion | flops 3145728 | bytes 8388608 | tf_op jit(solution)/shard_map/add | solution.py:61
  98.6 9.4 %all-gather.9.cloned.1.call-done = bf16[2,1024,1024]{2,1,0:T(8,128)(2,1)} async-done(((bf16[2,1024,512]{2,1,0:T(8,128)(2,1)}), bf16[2,1024,1024]{2,1,0:T(8,128)(2,1)}) %all-gather.9.cloned.1.call-update) | async-done | bytes 4194320 | tf_op jit(solution)/shard_map/all_gather | solution.py:57
  108.0 4.7 %fusion.13 = f32[2,512,1024]{2,1,0:T(8,128)S(1)} fusion(bf16[2,1024,512]{2,1,0:T(8,128)(2,1)S(1)} %bitcast.86, bf16[2,1024,1024]{2,1,0:T(8,128)(2,1)} %all-gather.9.cloned.1.call-done), kind=kOutput, calls=%fused_computation.39 | convolution fusion | flops 2147483648 | bytes 10485760 | tf_op jit(solution)/shard_map/sra,srb->sab/dot_general | solution.py:54
  112.8 1.9 copy-done.4
  114.7 8.2 %multiply_subtract_fusion.1 = f32[512,1024]{1,0:T(8,128)} fusion(f32[1024,1024]{1,0:T(8,128)S(1)} %copy-done, s32[]{:T(128)S(6)} %select_n.38, f32[2,512,1024]{2,1,0:T(8,128)S(1)} %fusion.13), kind=kOutput, calls=%fused_computation.11 | convolution fusion | flops 6443499520 | bytes 10485764 | tf_op jit(solution)/shard_map/dot_general | solution.py:68
  123.6 13.1 %gather_fusion.1 = bf16[2048]{0:T(1024)(128)(2,1)S(1)} fusion(bf16[2049]{0:T(1024)(128)(2,1)S(1)} %pad_maximum_fusion, s32[2048]{0:T(1024)S(1)} %fusion.5), kind=kCustom, calls=%fused_computation.1 | custom fusion | bytes 16384 | tf_op jit(solution)/shard_map/gather | solution.py:47
  137.4 6.4 %all-to-all-start.1 = ((bf16[2,16,64]{2,0,1:T(2,128)(2,1)}), bf16[2,16,64]{2,0,1:T(2,128)(2,1)S(1)}, u32[]{:S(2)}, u32[]{:S(2)}) async-start(bf16[2,16,64]{2,0,1:T(2,128)(2,1)} %copy.20), calls=%async_computation.1 | async-start | bytes 16384 | tf_op jit(solution)/shard_map/all_to_all | solution.py:50
  143.9 5.0 %all-to-all-done.1 = bf16[2,16,64]{2,0,1:T(2,128)(2,1)S(1)} async-done(((bf16[2,16,64]{2,0,1:T(2,128)(2,1)}), bf16[2,16,64]{2,0,1:T(2,128)(2,1)S(1)}, u32[]{:S(2)}, u32[]{:S(2)}) %all-to-all-start.1) | async-done | bytes 4128 | tf_op jit(solution)/shard_map/all_to_all | solution.py:50
  149.4 3.1 all-gather
  152.5 10.1 %multiply_subtract_fusion = f32[512,1024]{1,0:T(8,128)S(1)} fusion(f32[1024,1024]{1,0:T(8,128)} %convert_add_fusion, s32[]{:T(128)S(6)} %select_n.38, f32[2,512,1024]{2,1,0:T(8,128)} %copy-done.4), kind=kOutput, calls=%fused_computation.10 | convolution fusion | flops 6443499520 | bytes 10485764 | tf_op jit(solution)/shard_map/dot_general | solution.py:68
  164.0 1.9 fusion.8
  165.9 9.7 %fusion.14 = f32[512,1024]{1,0:T(8,128)S(1)} fusion(f32[512,1024]{1,0:T(8,128)} %copy-done.1, f32[1024,1024]{1,0:T(8,128)} %all-gather.11.cloned.1.call-done), kind=kOutput, calls=%fused_computation.40 | convolution fusion | flops 6442450944 | bytes 8388608 | tf_op jit(solution)/shard_map/dot_general | solution.py:18
  175.6 163.7 %while.12 = (s32[]{:T(128)}, f32[512]{0:T(512)S(1)}, pred[]{:T(512)}, f32[512,1024]{1,0:T(8,128)S(1)}, f32[512]{0:T(512)S(1)}, /*index=5*/f32[512]{0:T(512)S(1)}, s32[]{:T(128)}) while((s32[]{:T(128)}, f32[512]{0:T(512)S(1)}, pred[]{:T(512)}, f32[512,1024]{1,0:T(8,128)S(1)}, f32[512]{0:T(512)S(1)}, /*index=5*/f32[512]{0:T(512)S(1)}, ...), condition=%wide.region_5.6_spmd, body=%wide.region_4.5_spmd.sunk | while | flops 6292482 | bytes 2130038 | solution.py:91
  179.3 2.2 collective-permute-start
  181.5 3.9 %collective-permute-done = f32[512]{0:T(512)S(1)} collective-permute-done((f32[512]{0:T(512)S(1)}, f32[512]{0:T(512)S(1)}, u32[]{:S(2)}, u32[]{:S(2)}) %collective-permute-start) | collective-permute-done | bytes 2080 | tf_op jit(solution)/shard_map/while/body/eval_jaxpr/ppermute | solution.py:14
  185.4 3.0 all-gather.5
  190.3 1.9 collective-permute-start
  192.2 4.2 %collective-permute-done = f32[512]{0:T(512)S(1)} collective-permute-done((f32[512]{0:T(512)S(1)}, f32[512]{0:T(512)S(1)}, u32[]{:S(2)}, u32[]{:S(2)}) %collective-permute-start) | collective-permute-done | bytes 2080 | tf_op jit(solution)/shard_map/while/body/eval_jaxpr/ppermute | solution.py:14
  196.4 3.0 all-gather.5
  201.3 1.9 collective-permute-start
  203.2 4.2 %collective-permute-done = f32[512]{0:T(512)S(1)} collective-permute-done((f32[512]{0:T(512)S(1)}, f32[512]{0:T(512)S(1)}, u32[]{:S(2)}, u32[]{:S(2)}) %collective-permute-start) | collective-permute-done | bytes 2080 | tf_op jit(solution)/shard_map/while/body/eval_jaxpr/ppermute | solution.py:14
  207.4 3.0 all-gather.5
  212.2 1.9 collective-permute-start
  214.2 4.2 %collective-permute-done = f32[512]{0:T(512)S(1)} collective-permute-done((f32[512]{0:T(512)S(1)}, f32[512]{0:T(512)S(1)}, u32[]{:S(2)}, u32[]{:S(2)}) %collective-permute-start) | collective-permute-done | bytes 2080 | tf_op jit(solution)/shard_map/while/body/eval_jaxpr/ppermute | solution.py:14
  218.4 3.0 all-gather.5
  223.2 1.9 collective-permute-start
  225.2 4.2 %collective-permute-done = f32[512]{0:T(512)S(1)} collective-permute-done((f32[512]{0:T(512)S(1)}, f32[512]{0:T(512)S(1)}, u32[]{:S(2)}, u32[]{:S(2)}) %collective-permute-start) | collective-permute-done | bytes 2080 | tf_op jit(solution)/shard_map/while/body/eval_jaxpr/ppermute | solution.py:14
  229.4 3.0 all-gather.5
  234.2 1.9 collective-permute-start
  236.2 4.2 %collective-permute-done = f32[512]{0:T(512)S(1)} collective-permute-done((f32[512]{0:T(512)S(1)}, f32[512]{0:T(512)S(1)}, u32[]{:S(2)}, u32[]{:S(2)}) %collective-permute-start) | collective-permute-done | bytes 2080 | tf_op jit(solution)/shard_map/while/body/eval_jaxpr/ppermute | solution.py:14
  240.4 3.0 all-gather.5
  245.2 1.9 collective-permute-start
  247.1 4.2 %collective-permute-done = f32[512]{0:T(512)S(1)} collective-permute-done((f32[512]{0:T(512)S(1)}, f32[512]{0:T(512)S(1)}, u32[]{:S(2)}, u32[]{:S(2)}) %collective-permute-start) | collective-permute-done | bytes 2080 | tf_op jit(solution)/shard_map/while/body/eval_jaxpr/ppermute | solution.py:14
  251.3 3.0 all-gather.5
  256.2 1.9 collective-permute-start
  258.1 4.2 %collective-permute-done = f32[512]{0:T(512)S(1)} collective-permute-done((f32[512]{0:T(512)S(1)}, f32[512]{0:T(512)S(1)}, u32[]{:S(2)}, u32[]{:S(2)}) %collective-permute-start) | collective-permute-done | bytes 2080 | tf_op jit(solution)/shard_map/while/body/eval_jaxpr/ppermute | solution.py:14
  262.3 3.0 all-gather.5
  267.2 1.9 collective-permute-start
  269.1 4.2 %collective-permute-done = f32[512]{0:T(512)S(1)} collective-permute-done((f32[512]{0:T(512)S(1)}, f32[512]{0:T(512)S(1)}, u32[]{:S(2)}, u32[]{:S(2)}) %collective-permute-start) | collective-permute-done | bytes 2080 | tf_op jit(solution)/shard_map/while/body/eval_jaxpr/ppermute | solution.py:14
  273.3 3.0 all-gather.5
  278.2 1.9 collective-permute-start
  280.1 4.2 %collective-permute-done = f32[512]{0:T(512)S(1)} collective-permute-done((f32[512]{0:T(512)S(1)}, f32[512]{0:T(512)S(1)}, u32[]{:S(2)}, u32[]{:S(2)}) %collective-permute-start) | collective-permute-done | bytes 2080 | tf_op jit(solution)/shard_map/while/body/eval_jaxpr/ppermute | solution.py:14
  284.3 3.0 all-gather.5
  289.1 1.9 collective-permute-start
  291.1 4.2 %collective-permute-done = f32[512]{0:T(512)S(1)} collective-permute-done((f32[512]{0:T(512)S(1)}, f32[512]{0:T(512)S(1)}, u32[]{:S(2)}, u32[]{:S(2)}) %collective-permute-start) | collective-permute-done | bytes 2080 | tf_op jit(solution)/shard_map/while/body/eval_jaxpr/ppermute | solution.py:14
  295.3 3.0 all-gather.5
  300.1 1.9 collective-permute-start
  302.1 4.2 %collective-permute-done = f32[512]{0:T(512)S(1)} collective-permute-done((f32[512]{0:T(512)S(1)}, f32[512]{0:T(512)S(1)}, u32[]{:S(2)}, u32[]{:S(2)}) %collective-permute-start) | collective-permute-done | bytes 2080 | tf_op jit(solution)/shard_map/while/body/eval_jaxpr/ppermute | solution.py:14
  306.3 3.0 all-gather.5
  311.1 1.9 collective-permute-start
  313.1 4.2 %collective-permute-done = f32[512]{0:T(512)S(1)} collective-permute-done((f32[512]{0:T(512)S(1)}, f32[512]{0:T(512)S(1)}, u32[]{:S(2)}, u32[]{:S(2)}) %collective-permute-start) | collective-permute-done | bytes 2080 | tf_op jit(solution)/shard_map/while/body/eval_jaxpr/ppermute | solution.py:14
  317.3 3.0 all-gather.5
  322.1 1.9 collective-permute-start
  324.0 4.2 %collective-permute-done = f32[512]{0:T(512)S(1)} collective-permute-done((f32[512]{0:T(512)S(1)}, f32[512]{0:T(512)S(1)}, u32[]{:S(2)}, u32[]{:S(2)}) %collective-permute-start) | collective-permute-done | bytes 2080 | tf_op jit(solution)/shard_map/while/body/eval_jaxpr/ppermute | solution.py:14
  328.2 3.0 all-gather.5
  333.1 1.9 collective-permute-start
  335.0 4.2 %collective-permute-done = f32[512]{0:T(512)S(1)} collective-permute-done((f32[512]{0:T(512)S(1)}, f32[512]{0:T(512)S(1)}, u32[]{:S(2)}, u32[]{:S(2)}) %collective-permute-start) | collective-permute-done | bytes 2080 | tf_op jit(solution)/shard_map/while/body/eval_jaxpr/ppermute | solution.py:14
  339.2 3.1 all-gather.2
  342.3 3.4 fusion.16
  347.6 1.9 fusion.17
  (93 shorter events, 42.6 us)
Async XLA Ops:
  6.5 10.6 %copy-start.5 = (s32[2048,1]{0,1:T(1,128)S(1)}, s32[2048,1]{0,1:T(1,128)}, u32[]{:S(2)}) copy-start(s32[2048,1]{0,1:T(1,128)} %param.11) | copy-start | bytes 24580
  6.5 101.5 %all-gather.9.cloned.1.call-start = ((), (), s32[]{:S(2)}) async-start(), calls=%async_computation.2 | async-start | bytes 6291456 | tf_op jit(solution)/shard_map/all_gather | solution.py:57
  93.6 72.3 %all-gather.11.cloned.1.call-start = ((), (), s32[]{:S(2)}) async-start(), calls=%async_computation.3 | async-start | bytes 6291456 | tf_op jit(solution)/shard_map/all_gather | solution.py:77
  93.7 14.4 %copy-start.3 = (bf16[2,16,64,512]{3,2,1,0:T(8,128)(2,1)S(1)}, bf16[2,16,64,512]{3,2,1,0:T(8,128)(2,1)}, u32[]{:S(2)}) copy-start(bf16[2,16,64,512]{3,2,1,0:T(8,128)(2,1)} %copy.18) | copy-start | bytes 6291460
  108.0 6.7 %copy-start = (f32[1024,1024]{1,0:T(8,128)S(1)}, f32[1024,1024]{1,0:T(8,128)}, u32[]{:S(2)}) copy-start(f32[1024,1024]{1,0:T(8,128)} %convert_add_fusion) | copy-start | bytes 12582916
  112.7 2.0 copy-start.4
  123.0 0.7 copy-start.6
  123.6 20.2 %copy-start.7 = (f32[1024]{0:T(1024)S(1)}, f32[1024]{0:T(1024)}, u32[]{:S(2)}) copy-start(f32[1024]{0:T(1024)} %param.7) | copy-start | bytes 12292
  137.4 11.5 %all-to-all-start.1 = ((bf16[2,16,64]{2,0,1:T(2,128)(2,1)}), bf16[2,16,64]{2,0,1:T(2,128)(2,1)S(1)}, u32[]{:S(2)}, u32[]{:S(2)}) async-start(bf16[2,16,64]{2,0,1:T(2,128)(2,1)} %copy.20), calls=%async_computation.1 | async-start | bytes 16384 | tf_op jit(solution)/shard_map/all_to_all | solution.py:50
  162.7 1.3 copy-start.1
  179.3 6.1 %collective-permute-start = (f32[512]{0:T(512)S(1)}, f32[512]{0:T(512)S(1)}, u32[]{:S(2)}, u32[]{:S(2)}) collective-permute-start(f32[512]{0:T(512)S(1)} %add.85), channel_id=1, source_target_pairs={{0,2},{2,4},{4,6},{6,8},{8,10},{10,12},{12,14},{14,16},{16,18},{18... | collective-permute-start | bytes 6152 | tf_op jit(solution)/shard_map/while/body/eval_jaxpr/ppermute | solution.py:14
  190.3 6.1 %collective-permute-start = (f32[512]{0:T(512)S(1)}, f32[512]{0:T(512)S(1)}, u32[]{:S(2)}, u32[]{:S(2)}) collective-permute-start(f32[512]{0:T(512)S(1)} %add.85), channel_id=1, source_target_pairs={{0,2},{2,4},{4,6},{6,8},{8,10},{10,12},{12,14},{14,16},{16,18},{18... | collective-permute-start | bytes 6152 | tf_op jit(solution)/shard_map/while/body/eval_jaxpr/ppermute | solution.py:14
  201.3 6.1 %collective-permute-start = (f32[512]{0:T(512)S(1)}, f32[512]{0:T(512)S(1)}, u32[]{:S(2)}, u32[]{:S(2)}) collective-permute-start(f32[512]{0:T(512)S(1)} %add.85), channel_id=1, source_target_pairs={{0,2},{2,4},{4,6},{6,8},{8,10},{10,12},{12,14},{14,16},{16,18},{18... | collective-permute-start | bytes 6152 | tf_op jit(solution)/shard_map/while/body/eval_jaxpr/ppermute | solution.py:14
  212.2 6.1 %collective-permute-start = (f32[512]{0:T(512)S(1)}, f32[512]{0:T(512)S(1)}, u32[]{:S(2)}, u32[]{:S(2)}) collective-permute-start(f32[512]{0:T(512)S(1)} %add.85), channel_id=1, source_target_pairs={{0,2},{2,4},{4,6},{6,8},{8,10},{10,12},{12,14},{14,16},{16,18},{18... | collective-permute-start | bytes 6152 | tf_op jit(solution)/shard_map/while/body/eval_jaxpr/ppermute | solution.py:14
  223.2 6.1 %collective-permute-start = (f32[512]{0:T(512)S(1)}, f32[512]{0:T(512)S(1)}, u32[]{:S(2)}, u32[]{:S(2)}) collective-permute-start(f32[512]{0:T(512)S(1)} %add.85), channel_id=1, source_target_pairs={{0,2},{2,4},{4,6},{6,8},{8,10},{10,12},{12,14},{14,16},{16,18},{18... | collective-permute-start | bytes 6152 | tf_op jit(solution)/shard_map/while/body/eval_jaxpr/ppermute | solution.py:14
  234.2 6.1 %collective-permute-start = (f32[512]{0:T(512)S(1)}, f32[512]{0:T(512)S(1)}, u32[]{:S(2)}, u32[]{:S(2)}) collective-permute-start(f32[512]{0:T(512)S(1)} %add.85), channel_id=1, source_target_pairs={{0,2},{2,4},{4,6},{6,8},{8,10},{10,12},{12,14},{14,16},{16,18},{18... | collective-permute-start | bytes 6152 | tf_op jit(solution)/shard_map/while/body/eval_jaxpr/ppermute | solution.py:14
  245.2 6.1 %collective-permute-start = (f32[512]{0:T(512)S(1)}, f32[512]{0:T(512)S(1)}, u32[]{:S(2)}, u32[]{:S(2)}) collective-permute-start(f32[512]{0:T(512)S(1)} %add.85), channel_id=1, source_target_pairs={{0,2},{2,4},{4,6},{6,8},{8,10},{10,12},{12,14},{14,16},{16,18},{18... | collective-permute-start | bytes 6152 | tf_op jit(solution)/shard_map/while/body/eval_jaxpr/ppermute | solution.py:14
  256.2 6.1 %collective-permute-start = (f32[512]{0:T(512)S(1)}, f32[512]{0:T(512)S(1)}, u32[]{:S(2)}, u32[]{:S(2)}) collective-permute-start(f32[512]{0:T(512)S(1)} %add.85), channel_id=1, source_target_pairs={{0,2},{2,4},{4,6},{6,8},{8,10},{10,12},{12,14},{14,16},{16,18},{18... | collective-permute-start | bytes 6152 | tf_op jit(solution)/shard_map/while/body/eval_jaxpr/ppermute | solution.py:14
  267.2 6.1 %collective-permute-start = (f32[512]{0:T(512)S(1)}, f32[512]{0:T(512)S(1)}, u32[]{:S(2)}, u32[]{:S(2)}) collective-permute-start(f32[512]{0:T(512)S(1)} %add.85), channel_id=1, source_target_pairs={{0,2},{2,4},{4,6},{6,8},{8,10},{10,12},{12,14},{14,16},{16,18},{18... | collective-permute-start | bytes 6152 | tf_op jit(solution)/shard_map/while/body/eval_jaxpr/ppermute | solution.py:14
  278.2 6.1 %collective-permute-start = (f32[512]{0:T(512)S(1)}, f32[512]{0:T(512)S(1)}, u32[]{:S(2)}, u32[]{:S(2)}) collective-permute-start(f32[512]{0:T(512)S(1)} %add.85), channel_id=1, source_target_pairs={{0,2},{2,4},{4,6},{6,8},{8,10},{10,12},{12,14},{14,16},{16,18},{18... | collective-permute-start | bytes 6152 | tf_op jit(solution)/shard_map/while/body/eval_jaxpr/ppermute | solution.py:14
  289.1 6.1 %collective-permute-start = (f32[512]{0:T(512)S(1)}, f32[512]{0:T(512)S(1)}, u32[]{:S(2)}, u32[]{:S(2)}) collective-permute-start(f32[512]{0:T(512)S(1)} %add.85), channel_id=1, source_target_pairs={{0,2},{2,4},{4,6},{6,8},{8,10},{10,12},{12,14},{14,16},{16,18},{18... | collective-permute-start | bytes 6152 | tf_op jit(solution)/shard_map/while/body/eval_jaxpr/ppermute | solution.py:14
  300.1 6.1 %collective-permute-start = (f32[512]{0:T(512)S(1)}, f32[512]{0:T(512)S(1)}, u32[]{:S(2)}, u32[]{:S(2)}) collective-permute-start(f32[512]{0:T(512)S(1)} %add.85), channel_id=1, source_target_pairs={{0,2},{2,4},{4,6},{6,8},{8,10},{10,12},{12,14},{14,16},{16,18},{18... | collective-permute-start | bytes 6152 | tf_op jit(solution)/shard_map/while/body/eval_jaxpr/ppermute | solution.py:14
  311.1 6.1 %collective-permute-start = (f32[512]{0:T(512)S(1)}, f32[512]{0:T(512)S(1)}, u32[]{:S(2)}, u32[]{:S(2)}) collective-permute-start(f32[512]{0:T(512)S(1)} %add.85), channel_id=1, source_target_pairs={{0,2},{2,4},{4,6},{6,8},{8,10},{10,12},{12,14},{14,16},{16,18},{18... | collective-permute-start | bytes 6152 | tf_op jit(solution)/shard_map/while/body/eval_jaxpr/ppermute | solution.py:14
  322.1 6.1 %collective-permute-start = (f32[512]{0:T(512)S(1)}, f32[512]{0:T(512)S(1)}, u32[]{:S(2)}, u32[]{:S(2)}) collective-permute-start(f32[512]{0:T(512)S(1)} %add.85), channel_id=1, source_target_pairs={{0,2},{2,4},{4,6},{6,8},{8,10},{10,12},{12,14},{14,16},{16,18},{18... | collective-permute-start | bytes 6152 | tf_op jit(solution)/shard_map/while/body/eval_jaxpr/ppermute | solution.py:14
  333.1 6.1 %collective-permute-start = (f32[512]{0:T(512)S(1)}, f32[512]{0:T(512)S(1)}, u32[]{:S(2)}, u32[]{:S(2)}) collective-permute-start(f32[512]{0:T(512)S(1)} %add.85), channel_id=1, source_target_pairs={{0,2},{2,4},{4,6},{6,8},{8,10},{10,12},{12,14},{14,16},{16,18},{18... | collective-permute-start | bytes 6152 | tf_op jit(solution)/shard_map/while/body/eval_jaxpr/ppermute | solution.py:14
  339.2 8.4 %copy-start.2 = (f32[512,1024]{1,0:T(8,128)S(1)}, f32[512,1024]{1,0:T(8,128)}, u32[]{:S(2)}) copy-start(f32[512,1024]{1,0:T(8,128)} %copy-done.1) | copy-start | bytes 6291460
Sparse Core Ops, SparseCore 0:
  93.7 14.2 all-gather.8
  123.1 14.8 all-gather.10
where the time goes:
time: 358 us; the launch traced here: 357 us
  blocking collectives  105 us (29%)
  waiting for transfers between devices  77.1 us (22%)
  matrix products  68.2 us (19%)
  local copies, waits for them, and re-layouts  40.7 us (11%)
  starting transfers between devices  35.6 us (10%)
  other arithmetic  16.2 us (5%)
  between operations  13.6 us (4%)
    ppermute x15, waiting for transfers between devices, shifted(): lax.ppermute(value, axis, [(source, source + steps) for source in range(f...  62.7 us
    all_to_all x1, blocking collectives, body(): lax.all_to_all(send_rows, 'tm', split_axis=1, concat_axis=1, tiled=True)  53.8 us
    all_gather x15, blocking collectives, advance(): whole_state = lax.all_gather(state_rows, 'row', axis=0, tiled=True)  43.5 us
    ppermute x15, starting transfers between devices, shifted(): lax.ppermute(value, axis, [(source, source + steps) for source in range(f...  29.1 us
    dot_general x15, matrix products, advance(): jnp.dot(composed, whole_state, precision=lax.Precision.HIGHEST)  28 us
    dot_general x2, matrix products, body(): jnp.dot(information[slab_index], evolve, precision=lax.Precision.HIGHEST)  18.4 us
    gather x1, local copies, waits for them, and re-layouts, body(): padded_values[slot_table].reshape(SLAB_DEV, time_devs, capacity)  13.1 us
    dot_general x1, matrix products, left_product(): new_matrix = jnp.dot(left_rows, pieces[0], precision=lax.Precision.HIGHEST)  9.65 us
  transfers between devices with their start and end apart: 18, of which 17 were waited for; matrix products, arithmetic and copies ran while one was open for 9% of the time, Pallas kernels for 0%

commit v1 on v0

--- a/solution.py
+++ b/solution.py
@@ -2,6 +2,7 @@
 import jax.numpy as jnp
 from jax import lax
 from jax.sharding import PartitionSpec as P
+from jax.lax import all_to_all, axis_size
 
 SLAB_DEV = 2
 CAP = 64
@@ -46,7 +47,9 @@
     send_rows = padded_rows[slot_table].reshape(SLAB_DEV, time_devs, capacity, local_cols)
     send_values = padded_values[slot_table].reshape(SLAB_DEV, time_devs, capacity)
     recv_rows, recv_values = (
-        lax.all_to_all(send_rows, "tm", split_axis=1, concat_axis=1, tiled=True),
+        jnp.concatenate(
+            all_to_all(jnp.stack(jnp.split(send_rows, axis_size("tm"), axis=1)), "tm", 0, 0), axis=1
+        ),
         lax.all_to_all(send_values, "tm", split_axis=1, concat_axis=1, tiled=True),
     )
     slab_rows = recv_rows.reshape(SLAB_DEV, time_devs * capacity, local_cols)

time: 358 us -> 364 us (1.017)
  local copies, waits for them, and re-layouts: 40.7 us -> 46.5 us
    unnamed x17 -> x34, local copies, waits for them, and re-layouts: 3.97 us -> 11.6 us
where the time goes in v1:
time: 364 us; the launch traced here: 363 us
  blocking collectives  106 us (29%)
  waiting for transfers between devices  76.9 us (21%)
  matrix products  68.2 us (19%)
  local copies, waits for them, and re-layouts  46.5 us (13%)
  starting transfers between devices  35.8 us (10%)
  other arithmetic  16.2 us (4%)
  between operations  13.6 us (4%)
    ppermute x15, waiting for transfers between devices, shifted(): lax.ppermute(value, axis, [(source, source + steps) for source in range(f...  62.7 us
    all_to_all x1, blocking collectives, body(): all_to_all(jnp.stack(jnp.split(send_rows, axis_size('tm'), axis=1)), 'tm'...  53.8 us
    all_gather x15, blocking collectives, advance(): whole_state = lax.all_gather(state_rows, 'row', axis=0, tiled=True)  43.5 us
    ppermute x15, starting transfers between devices, shifted(): lax.ppermute(value, axis, [(source, source + steps) for source in range(f...  29.1 us
    dot_general x15, matrix products, advance(): jnp.dot(composed, whole_state, precision=lax.Precision.HIGHEST)  28 us
    dot_general x2, matrix products, body(): jnp.dot(information[slab_index], evolve, precision=lax.Precision.HIGHEST)  18.4 us
    gather x1, local copies, waits for them, and re-layouts, body(): padded_values[slot_table].reshape(SLAB_DEV, time_devs, capacity)  13.1 us
    unnamed x34, local copies, waits for them, and re-layouts  11.6 us
  transfers between devices with their start and end apart: 18, of which 17 were waited for; matrix products, arithmetic and copies ran while one was open for 9% of the time, Pallas kernels for 0%

profile of v1, /device:TPU:9, one launch (start us, length us, event | category | flops | bytes accessed | tf_op | source)
XLA Modules:
  0.0 363.0 jit_solution(17604616806247130671)
XLA Ops:
  7.3 9.1 %reduce-window.6 = s32[32,16,128]{2,1,0:T(8,128)S(1)} reduce-window(s32[32,16,128]{2,1,0:T(8,128)S(1)} %fusion.4, s32[]{:T(128)} %copy.130), window={size=1x1x128 pad=0_0x0_0x127_0}, to_apply=%region_0.0 | reduce-window | flops 8323072 | bytes 524292 | tf_op jit(solution)/shard_map/reduce-window
  17.3 8.0 %scatter_custom_fusion = s32[2048]{0:T(1024)S(1)} fusion(s32[2048]{0:T(1024)S(1)} %bitcast.223, s32[2048]{0:T(1024)S(1)} %iota.23, s32[]{:T(128)} %constant.63.clone.1), kind=kCustom, calls=%fused_computation.66 | custom fusion | bytes 8196 | tf_op jit(solution)/shard_map/scatter | solution.py:43
  27.1 9.2 %gather_fusion = bf16[2048,512]{1,0:T(8,128)(2,1)} fusion(bf16[2049,512]{1,0:T(8,128)(2,1)S(1)} %concatenate.6, s32[2048]{0:T(1024)S(1)} %fusion.21), kind=kCustom, calls=%fused_computation | custom fusion | bytes 4202496 | tf_op jit(solution)/shard_map/gather | solution.py:47
  44.0 53.8 %all_to_all.10 = bf16[16,2,1,64,512]{4,3,1,2,0:T(8,128)(2,1)S(1)} all-to-all(bf16[16,2,1,64,512]{4,3,1,2,0:T(8,128)(2,1)S(1)} %fusion.5), channel_id=1, replica_groups=mesh['tm'=16,'row'=2] {'tm'}, dimensions={0} | all-to-all | bytes 4194304 | tf_op jit(solution)/shard_map/all_to_all | solution.py:51
  99.7 5.0 %convert_add_fusion = f32[1024,1024]{1,0:T(8,128)} fusion(f32[1024,1024]{1,0:T(8,128)} %param.8), kind=kLoop, calls=%fused_computation.4 | loop fusion | flops 3145728 | bytes 8388608 | tf_op jit(solution)/shard_map/add | solution.py:64
  104.7 9.2 %all-gather.9.cloned.1.call-done = bf16[2,1024,1024]{2,1,0:T(8,128)(2,1)} async-done(((bf16[2,1024,512]{2,1,0:T(8,128)(2,1)}), bf16[2,1024,1024]{2,1,0:T(8,128)(2,1)}) %all-gather.9.cloned.1.call-update) | async-done | bytes 4194320 | tf_op jit(solution)/shard_map/all_gather | solution.py:60
  113.9 4.7 %fusion.29 = f32[2,512,1024]{2,1,0:T(8,128)S(1)} fusion(bf16[2,1024,512]{2,1,0:T(8,128)(2,1)S(1)} %bitcast.183, bf16[2,1024,1024]{2,1,0:T(8,128)(2,1)} %all-gather.9.cloned.1.call-done), kind=kOutput, calls=%fused_computation.71 | convolution fusion | flops 2147483648 | bytes 10485760 | tf_op jit(solution)/shard_map/sra,srb->sab/dot_general | solution.py:57
  118.6 2.0 copy-done.5
  120.6 8.3 %multiply_subtract_fusion.1 = f32[512,1024]{1,0:T(8,128)} fusion(f32[1024,1024]{1,0:T(8,128)S(1)} %copy-done, s32[]{:T(128)S(6)} %select_n.38, f32[2,512,1024]{2,1,0:T(8,128)S(1)} %fusion.29), kind=kOutput, calls=%fused_computation.11 | convolution fusion | flops 6443499520 | bytes 10485764 | tf_op jit(solution)/shard_map/dot_general | solution.py:71
  129.5 13.1 %gather_fusion.1 = bf16[2048]{0:T(1024)(128)(2,1)S(1)} fusion(bf16[2049]{0:T(1024)(128)(2,1)S(1)} %pad_maximum_fusion, s32[2048]{0:T(1024)S(1)} %fusion.21), kind=kCustom, calls=%fused_computation.1 | custom fusion | bytes 16384 | tf_op jit(solution)/shard_map/gather | solution.py:48
  143.3 6.4 %all-to-all-start.1 = ((bf16[2,16,64]{2,0,1:T(2,128)(2,1)}), bf16[2,16,64]{2,0,1:T(2,128)(2,1)S(1)}, u32[]{:S(2)}, u32[]{:S(2)}) async-start(bf16[2,16,64]{2,0,1:T(2,128)(2,1)} %copy.82), calls=%async_computation.1 | async-start | bytes 16384 | tf_op jit(solution)/shard_map/all_to_all | solution.py:53
  149.8 5.0 %all-to-all-done.1 = bf16[2,16,64]{2,0,1:T(2,128)(2,1)S(1)} async-done(((bf16[2,16,64]{2,0,1:T(2,128)(2,1)}), bf16[2,16,64]{2,0,1:T(2,128)(2,1)S(1)}, u32[]{:S(2)}, u32[]{:S(2)}) %all-to-all-start.1) | async-done | bytes 4128 | tf_op jit(solution)/shard_map/all_to_all | solution.py:53
  155.3 3.4 all-gather
  158.6 10.1 %multiply_subtract_fusion = f32[512,1024]{1,0:T(8,128)S(1)} fusion(f32[1024,1024]{1,0:T(8,128)} %convert_add_fusion, s32[]{:T(128)S(6)} %select_n.38, f32[2,512,1024]{2,1,0:T(8,128)} %copy-done.5), kind=kOutput, calls=%fused_computation.10 | convolution fusion | flops 6443499520 | bytes 10485764 | tf_op jit(solution)/shard_map/dot_general | solution.py:71
  170.1 1.9 fusion.24
  172.0 9.7 %fusion.30 = f32[512,1024]{1,0:T(8,128)S(1)} fusion(f32[512,1024]{1,0:T(8,128)} %copy-done.1, f32[1024,1024]{1,0:T(8,128)} %all-gather.11.cloned.1.call-done), kind=kOutput, calls=%fused_computation.72 | convolution fusion | flops 6442450944 | bytes 8388608 | tf_op jit(solution)/shard_map/dot_general | solution.py:19
  181.6 163.7 %while.12 = (s32[]{:T(128)}, f32[512]{0:T(512)S(1)}, pred[]{:T(512)}, f32[512,1024]{1,0:T(8,128)S(1)}, f32[512]{0:T(512)S(1)}, /*index=5*/f32[512]{0:T(512)S(1)}, s32[]{:T(128)}) while((s32[]{:T(128)}, f32[512]{0:T(512)S(1)}, pred[]{:T(512)}, f32[512,1024]{1,0:T(8,128)S(1)}, f32[512]{0:T(512)S(1)}, /*index=5*/f32[512]{0:T(512)S(1)}, ...), condition=%wide.region_5.6_spmd, body=%wide.region_4.5_spmd.sunk | while | flops 6292482 | bytes 2130038 | solution.py:94
  185.4 2.2 collective-permute-start
  187.6 3.9 %collective-permute-done = f32[512]{0:T(512)S(1)} collective-permute-done((f32[512]{0:T(512)S(1)}, f32[512]{0:T(512)S(1)}, u32[]{:S(2)}, u32[]{:S(2)}) %collective-permute-start) | collective-permute-done | bytes 2080 | tf_op jit(solution)/shard_map/while/body/eval_jaxpr/ppermute | solution.py:15
  191.5 3.0 all-gather.5
  196.4 1.9 collective-permute-start
  198.3 4.2 %collective-permute-done = f32[512]{0:T(512)S(1)} collective-permute-done((f32[512]{0:T(512)S(1)}, f32[512]{0:T(512)S(1)}, u32[]{:S(2)}, u32[]{:S(2)}) %collective-permute-start) | collective-permute-done | bytes 2080 | tf_op jit(solution)/shard_map/while/body/eval_jaxpr/ppermute | solution.py:15
  202.5 3.0 all-gather.5
  207.3 1.9 collective-permute-start
  209.3 4.2 %collective-permute-done = f32[512]{0:T(512)S(1)} collective-permute-done((f32[512]{0:T(512)S(1)}, f32[512]{0:T(512)S(1)}, u32[]{:S(2)}, u32[]{:S(2)}) %collective-permute-start) | collective-permute-done | bytes 2080 | tf_op jit(solution)/shard_map/while/body/eval_jaxpr/ppermute | solution.py:15
  213.5 3.0 all-gather.5
  218.3 1.9 collective-permute-start
  220.3 4.2 %collective-permute-done = f32[512]{0:T(512)S(1)} collective-permute-done((f32[512]{0:T(512)S(1)}, f32[512]{0:T(512)S(1)}, u32[]{:S(2)}, u32[]{:S(2)}) %collective-permute-start) | collective-permute-done | bytes 2080 | tf_op jit(solution)/shard_map/while/body/eval_jaxpr/ppermute | solution.py:15
  224.5 3.0 all-gather.5
  229.3 1.9 collective-permute-start
  231.2 4.2 %collective-permute-done = f32[512]{0:T(512)S(1)} collective-permute-done((f32[512]{0:T(512)S(1)}, f32[512]{0:T(512)S(1)}, u32[]{:S(2)}, u32[]{:S(2)}) %collective-permute-start) | collective-permute-done | bytes 2080 | tf_op jit(solution)/shard_map/while/body/eval_jaxpr/ppermute | solution.py:15
  235.5 3.0 all-gather.5
  240.3 1.9 collective-permute-start
  242.2 4.2 %collective-permute-done = f32[512]{0:T(512)S(1)} collective-permute-done((f32[512]{0:T(512)S(1)}, f32[512]{0:T(512)S(1)}, u32[]{:S(2)}, u32[]{:S(2)}) %collective-permute-start) | collective-permute-done | bytes 2080 | tf_op jit(solution)/shard_map/while/body/eval_jaxpr/ppermute | solution.py:15
  246.4 3.0 all-gather.5
  251.3 1.9 collective-permute-start
  253.2 4.2 %collective-permute-done = f32[512]{0:T(512)S(1)} collective-permute-done((f32[512]{0:T(512)S(1)}, f32[512]{0:T(512)S(1)}, u32[]{:S(2)}, u32[]{:S(2)}) %collective-permute-start) | collective-permute-done | bytes 2080 | tf_op jit(solution)/shard_map/while/body/eval_jaxpr/ppermute | solution.py:15
  257.4 3.0 all-gather.5
  262.3 1.9 collective-permute-start
  264.2 4.2 %collective-permute-done = f32[512]{0:T(512)S(1)} collective-permute-done((f32[512]{0:T(512)S(1)}, f32[512]{0:T(512)S(1)}, u32[]{:S(2)}, u32[]{:S(2)}) %collective-permute-start) | collective-permute-done | bytes 2080 | tf_op jit(solution)/shard_map/while/body/eval_jaxpr/ppermute | solution.py:15
  268.4 3.0 all-gather.5
  273.3 1.9 collective-permute-start
  275.2 4.2 %collective-permute-done = f32[512]{0:T(512)S(1)} collective-permute-done((f32[512]{0:T(512)S(1)}, f32[512]{0:T(512)S(1)}, u32[]{:S(2)}, u32[]{:S(2)}) %collective-permute-start) | collective-permute-done | bytes 2080 | tf_op jit(solution)/shard_map/while/body/eval_jaxpr/ppermute | solution.py:15
  279.4 3.0 all-gather.5
  284.2 1.9 collective-permute-start
  286.2 4.2 %collective-permute-done = f32[512]{0:T(512)S(1)} collective-permute-done((f32[512]{0:T(512)S(1)}, f32[512]{0:T(512)S(1)}, u32[]{:S(2)}, u32[]{:S(2)}) %collective-permute-start) | collective-permute-done | bytes 2080 | tf_op jit(solution)/shard_map/while/body/eval_jaxpr/ppermute | solution.py:15
  290.4 3.0 all-gather.5
  295.2 1.9 collective-permute-start
  297.2 4.2 %collective-permute-done = f32[512]{0:T(512)S(1)} collective-permute-done((f32[512]{0:T(512)S(1)}, f32[512]{0:T(512)S(1)}, u32[]{:S(2)}, u32[]{:S(2)}) %collective-permute-start) | collective-permute-done | bytes 2080 | tf_op jit(solution)/shard_map/while/body/eval_jaxpr/ppermute | solution.py:15
  301.4 3.0 all-gather.5
  306.2 1.9 collective-permute-start
  308.2 4.2 %collective-permute-done = f32[512]{0:T(512)S(1)} collective-permute-done((f32[512]{0:T(512)S(1)}, f32[512]{0:T(512)S(1)}, u32[]{:S(2)}, u32[]{:S(2)}) %collective-permute-start) | collective-permute-done | bytes 2080 | tf_op jit(solution)/shard_map/while/body/eval_jaxpr/ppermute | solution.py:15
  312.4 3.0 all-gather.5
  317.2 1.9 collective-permute-start
  319.1 4.2 %collective-permute-done = f32[512]{0:T(512)S(1)} collective-permute-done((f32[512]{0:T(512)S(1)}, f32[512]{0:T(512)S(1)}, u32[]{:S(2)}, u32[]{:S(2)}) %collective-permute-start) | collective-permute-done | bytes 2080 | tf_op jit(solution)/shard_map/while/body/eval_jaxpr/ppermute | solution.py:15
  323.3 3.0 all-gather.5
  328.2 1.9 collective-permute-start
  330.1 4.2 %collective-permute-done = f32[512]{0:T(512)S(1)} collective-permute-done((f32[512]{0:T(512)S(1)}, f32[512]{0:T(512)S(1)}, u32[]{:S(2)}, u32[]{:S(2)}) %collective-permute-start) | collective-permute-done | bytes 2080 | tf_op jit(solution)/shard_map/while/body/eval_jaxpr/ppermute | solution.py:15
  334.3 3.0 all-gather.5
  339.2 1.9 collective-permute-start
  341.1 4.2 %collective-permute-done = f32[512]{0:T(512)S(1)} collective-permute-done((f32[512]{0:T(512)S(1)}, f32[512]{0:T(512)S(1)}, u32[]{:S(2)}, u32[]{:S(2)}) %collective-permute-start) | collective-permute-done | bytes 2080 | tf_op jit(solution)/shard_map/while/body/eval_jaxpr/ppermute | solution.py:15
  345.3 3.1 all-gather.2
  348.4 3.4 fusion.32
  353.7 1.9 fusion.33
  (110 shorter events, 48.6 us)
Async XLA Ops:
  6.5 10.6 %copy-start.6 = (s32[2048,1]{0,1:T(1,128)S(1)}, s32[2048,1]{0,1:T(1,128)}, u32[]{:S(2)}) copy-start(s32[2048,1]{0,1:T(1,128)} %param.11) | copy-start | bytes 24580
  6.5 107.3 %all-gather.9.cloned.1.call-start = ((), (), s32[]{:S(2)}) async-start(), calls=%async_computation.2 | async-start | bytes 6291456 | tf_op jit(solution)/shard_map/all_gather | solution.py:60
  36.3 7.5 %copy-start.4 = (bf16[2048,512]{1,0:T(8,128)(2,1)S(1)}, bf16[2048,512]{1,0:T(8,128)(2,1)}, u32[]{:S(2)}) copy-start(bf16[2048,512]{1,0:T(8,128)(2,1)} %gather_fusion) | copy-start | bytes 6291460
  99.5 72.5 %all-gather.11.cloned.1.call-start = ((), (), s32[]{:S(2)}) async-start(), calls=%async_computation.3 | async-start | bytes 6291456 | tf_op jit(solution)/shard_map/all_gather | solution.py:80
  99.7 14.2 %copy-start.3 = (bf16[2,16,1,64,512]{4,3,1,0,2:T(8,128)(2,1)S(1)}, bf16[2,16,1,64,512]{4,3,1,0,2:T(8,128)(2,1)}, u32[]{:S(2)}) copy-start(bf16[2,16,1,64,512]{4,3,1,0,2:T(8,128)(2,1)} %copy.80) | copy-start | bytes 6291460
  113.9 6.7 %copy-start = (f32[1024,1024]{1,0:T(8,128)S(1)}, f32[1024,1024]{1,0:T(8,128)}, u32[]{:S(2)}) copy-start(f32[1024,1024]{1,0:T(8,128)} %convert_add_fusion) | copy-start | bytes 12582916
  118.6 2.0 copy-start.5
  128.8 0.7 copy-start.7
  129.5 20.2 %copy-start.8 = (f32[1024]{0:T(1024)S(1)}, f32[1024]{0:T(1024)}, u32[]{:S(2)}) copy-start(f32[1024]{0:T(1024)} %param.7) | copy-start | bytes 12292
  143.3 11.5 %all-to-all-start.1 = ((bf16[2,16,64]{2,0,1:T(2,128)(2,1)}), bf16[2,16,64]{2,0,1:T(2,128)(2,1)S(1)}, u32[]{:S(2)}, u32[]{:S(2)}) async-start(bf16[2,16,64]{2,0,1:T(2,128)(2,1)} %copy.82), calls=%async_computation.1 | async-start | bytes 16384 | tf_op jit(solution)/shard_map/all_to_all | solution.py:53
  168.8 1.3 copy-start.1
  185.4 6.1 %collective-permute-start = (f32[512]{0:T(512)S(1)}, f32[512]{0:T(512)S(1)}, u32[]{:S(2)}, u32[]{:S(2)}) collective-permute-start(f32[512]{0:T(512)S(1)} %add.85), channel_id=1, source_target_pairs={{0,2},{2,4},{4,6},{6,8},{8,10},{10,12},{12,14},{14,16},{16,18},{18... | collective-permute-start | bytes 6152 | tf_op jit(solution)/shard_map/while/body/eval_jaxpr/ppermute | solution.py:15
  196.4 6.1 %collective-permute-start = (f32[512]{0:T(512)S(1)}, f32[512]{0:T(512)S(1)}, u32[]{:S(2)}, u32[]{:S(2)}) collective-permute-start(f32[512]{0:T(512)S(1)} %add.85), channel_id=1, source_target_pairs={{0,2},{2,4},{4,6},{6,8},{8,10},{10,12},{12,14},{14,16},{16,18},{18... | collective-permute-start | bytes 6152 | tf_op jit(solution)/shard_map/while/body/eval_jaxpr/ppermute | solution.py:15
  207.3 6.1 %collective-permute-start = (f32[512]{0:T(512)S(1)}, f32[512]{0:T(512)S(1)}, u32[]{:S(2)}, u32[]{:S(2)}) collective-permute-start(f32[512]{0:T(512)S(1)} %add.85), channel_id=1, source_target_pairs={{0,2},{2,4},{4,6},{6,8},{8,10},{10,12},{12,14},{14,16},{16,18},{18... | collective-permute-start | bytes 6152 | tf_op jit(solution)/shard_map/while/body/eval_jaxpr/ppermute | solution.py:15
  218.3 6.1 %collective-permute-start = (f32[512]{0:T(512)S(1)}, f32[512]{0:T(512)S(1)}, u32[]{:S(2)}, u32[]{:S(2)}) collective-permute-start(f32[512]{0:T(512)S(1)} %add.85), channel_id=1, source_target_pairs={{0,2},{2,4},{4,6},{6,8},{8,10},{10,12},{12,14},{14,16},{16,18},{18... | collective-permute-start | bytes 6152 | tf_op jit(solution)/shard_map/while/body/eval_jaxpr/ppermute | solution.py:15
  229.3 6.1 %collective-permute-start = (f32[512]{0:T(512)S(1)}, f32[512]{0:T(512)S(1)}, u32[]{:S(2)}, u32[]{:S(2)}) collective-permute-start(f32[512]{0:T(512)S(1)} %add.85), channel_id=1, source_target_pairs={{0,2},{2,4},{4,6},{6,8},{8,10},{10,12},{12,14},{14,16},{16,18},{18... | collective-permute-start | bytes 6152 | tf_op jit(solution)/shard_map/while/body/eval_jaxpr/ppermute | solution.py:15
  240.3 6.1 %collective-permute-start = (f32[512]{0:T(512)S(1)}, f32[512]{0:T(512)S(1)}, u32[]{:S(2)}, u32[]{:S(2)}) collective-permute-start(f32[512]{0:T(512)S(1)} %add.85), channel_id=1, source_target_pairs={{0,2},{2,4},{4,6},{6,8},{8,10},{10,12},{12,14},{14,16},{16,18},{18... | collective-permute-start | bytes 6152 | tf_op jit(solution)/shard_map/while/body/eval_jaxpr/ppermute | solution.py:15
  251.3 6.1 %collective-permute-start = (f32[512]{0:T(512)S(1)}, f32[512]{0:T(512)S(1)}, u32[]{:S(2)}, u32[]{:S(2)}) collective-permute-start(f32[512]{0:T(512)S(1)} %add.85), channel_id=1, source_target_pairs={{0,2},{2,4},{4,6},{6,8},{8,10},{10,12},{12,14},{14,16},{16,18},{18... | collective-permute-start | bytes 6152 | tf_op jit(solution)/shard_map/while/body/eval_jaxpr/ppermute | solution.py:15
  262.3 6.1 %collective-permute-start = (f32[512]{0:T(512)S(1)}, f32[512]{0:T(512)S(1)}, u32[]{:S(2)}, u32[]{:S(2)}) collective-permute-start(f32[512]{0:T(512)S(1)} %add.85), channel_id=1, source_target_pairs={{0,2},{2,4},{4,6},{6,8},{8,10},{10,12},{12,14},{14,16},{16,18},{18... | collective-permute-start | bytes 6152 | tf_op jit(solution)/shard_map/while/body/eval_jaxpr/ppermute | solution.py:15
  273.3 6.1 %collective-permute-start = (f32[512]{0:T(512)S(1)}, f32[512]{0:T(512)S(1)}, u32[]{:S(2)}, u32[]{:S(2)}) collective-permute-start(f32[512]{0:T(512)S(1)} %add.85), channel_id=1, source_target_pairs={{0,2},{2,4},{4,6},{6,8},{8,10},{10,12},{12,14},{14,16},{16,18},{18... | collective-permute-start | bytes 6152 | tf_op jit(solution)/shard_map/while/body/eval_jaxpr/ppermute | solution.py:15
  284.2 6.1 %collective-permute-start = (f32[512]{0:T(512)S(1)}, f32[512]{0:T(512)S(1)}, u32[]{:S(2)}, u32[]{:S(2)}) collective-permute-start(f32[512]{0:T(512)S(1)} %add.85), channel_id=1, source_target_pairs={{0,2},{2,4},{4,6},{6,8},{8,10},{10,12},{12,14},{14,16},{16,18},{18... | collective-permute-start | bytes 6152 | tf_op jit(solution)/shard_map/while/body/eval_jaxpr/ppermute | solution.py:15
  295.2 6.1 %collective-permute-start = (f32[512]{0:T(512)S(1)}, f32[512]{0:T(512)S(1)}, u32[]{:S(2)}, u32[]{:S(2)}) collective-permute-start(f32[512]{0:T(512)S(1)} %add.85), channel_id=1, source_target_pairs={{0,2},{2,4},{4,6},{6,8},{8,10},{10,12},{12,14},{14,16},{16,18},{18... | collective-permute-start | bytes 6152 | tf_op jit(solution)/shard_map/while/body/eval_jaxpr/ppermute | solution.py:15
  306.2 6.1 %collective-permute-start = (f32[512]{0:T(512)S(1)}, f32[512]{0:T(512)S(1)}, u32[]{:S(2)}, u32[]{:S(2)}) collective-permute-start(f32[512]{0:T(512)S(1)} %add.85), channel_id=1, source_target_pairs={{0,2},{2,4},{4,6},{6,8},{8,10},{10,12},{12,14},{14,16},{16,18},{18... | collective-permute-start | bytes 6152 | tf_op jit(solution)/shard_map/while/body/eval_jaxpr/ppermute | solution.py:15
  317.2 6.1 %collective-permute-start = (f32[512]{0:T(512)S(1)}, f32[512]{0:T(512)S(1)}, u32[]{:S(2)}, u32[]{:S(2)}) collective-permute-start(f32[512]{0:T(512)S(1)} %add.85), channel_id=1, source_target_pairs={{0,2},{2,4},{4,6},{6,8},{8,10},{10,12},{12,14},{14,16},{16,18},{18... | collective-permute-start | bytes 6152 | tf_op jit(solution)/shard_map/while/body/eval_jaxpr/ppermute | solution.py:15
  328.2 6.1 %collective-permute-start = (f32[512]{0:T(512)S(1)}, f32[512]{0:T(512)S(1)}, u32[]{:S(2)}, u32[]{:S(2)}) collective-permute-start(f32[512]{0:T(512)S(1)} %add.85), channel_id=1, source_target_pairs={{0,2},{2,4},{4,6},{6,8},{8,10},{10,12},{12,14},{14,16},{16,18},{18... | collective-permute-start | bytes 6152 | tf_op jit(solution)/shard_map/while/body/eval_jaxpr/ppermute | solution.py:15
  339.2 6.1 %collective-permute-start = (f32[512]{0:T(512)S(1)}, f32[512]{0:T(512)S(1)}, u32[]{:S(2)}, u32[]{:S(2)}) collective-permute-start(f32[512]{0:T(512)S(1)} %add.85), channel_id=1, source_target_pairs={{0,2},{2,4},{4,6},{6,8},{8,10},{10,12},{12,14},{14,16},{16,18},{18... | collective-permute-start | bytes 6152 | tf_op jit(solution)/shard_map/while/body/eval_jaxpr/ppermute | solution.py:15
  345.3 8.4 %copy-start.2 = (f32[512,1024]{1,0:T(8,128)S(1)}, f32[512,1024]{1,0:T(8,128)}, u32[]{:S(2)}) copy-start(f32[512,1024]{1,0:T(8,128)} %copy-done.1) | copy-start | bytes 6291460
Sparse Core Ops, SparseCore 0:
  99.6 14.2 all-gather.8
  129.0 14.8 all-gather.10
